TPU v7x, 128 devices: a whole 4x4x4 slice. The times are simulated.
128 devices in a mesh: dp: 16 (over y, z), ctx: 8 (over x, core).
Axes of the slice: x: 4, y: 4, z: 4, core: 2. Of those that a mesh axis runs over, the one named last changes fastest.
Arguments:
- input_entries: bfloat16 [16, 2048, 8192], P('dp', 'ctx'), may hold values from -6 to 6
- segment_entry_counts: int32 [16, 8, 8], P('dp'), may hold values from 1 to 64, as said below
- segment_destination_part: int32 [16, 8, 8], P('dp'), may hold values from 0 to 7, as said below
- norm_gain: float32 [8192], replicated, may hold values from 0.25 to 1.75
- kv_weight: bfloat16 [8192, 2048], P('dp'), may hold values from -0.0625 to 0.0625
- kv_bias: float32 [2048], replicated, may hold values from -3 to 3
Outputs:
- evened_residual_entries: bfloat16 [16, 2048, 8192], P('dp', 'ctx')
- lookup_stored_tensors: bfloat16 [16, 2048, 2, 8, 128], P('dp', None, None, 'ctx')
Inputs may be any that keep to these rules, and one draw needn't show every extreme that they name: `segment_entry_counts`: in each sequence the runs of one shard cover its 256 rows; every shard receives exactly 256 rows; at most 64 rows go from one shard to one shard, and every sequence has a run of exactly 64. The numbers of rows between shards form a Latin arrangement: every shard sends the same list of 8 numbers, one to each shard, and receives each number of that list once. `segment_destination_part`: the 8 runs of one shard go to 8 different shards.
All inputs are finite; a program needn't handle non-finite values.
Results may differ from a plain program's by a relative error of at most 0.0046.
Values may be sent and summed in bfloat16 or wider, within the bound.
A program may use at most 192 MiB of HBM per device.

v0:
```python
import jax
import jax.numpy as jnp
from jax import lax
from jax.sharding import PartitionSpec as P

KVH = 8
HD = 128


def plan_tables(lengths, targets, peer_count):
    labels = jnp.arange(peer_count, dtype=jnp.int32)
    starts = jnp.cumsum(lengths, axis=1) - lengths
    matches = (targets[:, :, None] == labels[None, None, :]).astype(jnp.int32)
    counts = jnp.sum(lengths[:, :, None] * matches, axis=1)
    anchors = jnp.sum(starts[:, :, None] * matches, axis=1)
    run_ends = jnp.cumsum(counts, axis=0)
    offsets = run_ends - counts
    return (counts, anchors, offsets, run_ends)


def source_of(positions, ends_column, offsets_column, anchors_column, peer_count):
    labels = jnp.arange(peer_count, dtype=jnp.int32)
    source = jnp.sum((ends_column[None, :] <= positions[:, None]).astype(jnp.int32), axis=1)
    chosen = (source[:, None] == labels[None, :]).astype(jnp.int32)
    within = positions - jnp.sum(chosen * offsets_column[None, :], axis=1)
    anchor = jnp.sum(chosen * anchors_column[None, :], axis=1)
    return (source, within, anchor)


def rms_normed(rows, norm_gain):
    as_float = rows.astype(jnp.float32)
    inverse_rms = lax.rsqrt(jnp.mean(as_float * as_float, axis=-1, keepdims=True) + 1e-06)
    return (as_float * inverse_rms * norm_gain[None, :]).astype(jnp.bfloat16)


def pack_document_runs(rows, counts, anchors, myself, peer_count):
    row_count = rows.shape[0]
    capacity = 2 * row_count // peer_count
    slot_index = jnp.arange(capacity, dtype=jnp.int32)
    my_counts = counts[myself]
    my_anchors = anchors[myself]
    wanted = jnp.minimum(my_anchors[:, None] + slot_index[None, :], row_count - 1)
    is_live = slot_index[None, :] < my_counts[:, None]
    picked = jnp.take(rows, wanted.reshape(-1), axis=0).reshape(peer_count, capacity, -1)
    return jnp.where(is_live[:, :, None], picked, jnp.zeros_like(picked))


def unpack_runs(arriving_rows, positions, run_ends, offsets, anchors, myself, peer_count):
    capacity = arriving_rows.shape[1]
    source, within, anchor = source_of(
        positions, run_ends[:, myself], offsets[:, myself], anchors[:, myself], peer_count
    )
    flat_rows = arriving_rows.reshape(peer_count * capacity, -1)
    return jnp.take(flat_rows, source * capacity + within, axis=0)


def on_device(
    input_entries, segment_entry_counts, segment_destination_part, norm_gain, kv_weight, kv_bias
):
    peer_count = lax.axis_size("ctx")
    myself = lax.axis_index("ctx")
    row_count = input_entries.shape[1]
    counts, anchors, offsets, run_ends = plan_tables(
        segment_entry_counts[0], segment_destination_part[0], peer_count
    )
    positions = jnp.arange(row_count, dtype=jnp.int32)
    outgoing = pack_document_runs(input_entries[0], counts, anchors, myself, peer_count)
    arriving_rows = lax.all_to_all(outgoing, "ctx", split_axis=0, concat_axis=0, tiled=True)
    moved_rows = unpack_runs(
        arriving_rows, positions, run_ends, offsets, anchors, myself, peer_count
    )
    normed = rms_normed(moved_rows, norm_gain)
    summed_squares = jnp.dot(
        normed,
        lax.all_gather(kv_weight, "dp", axis=0, tiled=True),
        preferred_element_type=jnp.float32,
    )
    mapped_outputs = (
        (summed_squares + kv_bias[None, :]).astype(jnp.bfloat16).reshape(1, row_count, 2, KVH, HD)
    )
    by_heads = lax.all_to_all(mapped_outputs, "ctx", split_axis=3, concat_axis=1, tiled=True)
    return (moved_rows[None], by_heads)


def solution(mesh):
    in_specs = (
        P("dp", "ctx", None),
        P("dp", None, None),
        P("dp", None, None),
        P(),
        P("dp", None),
        P(),
    )
    out_specs = (P("dp", "ctx", None), P("dp", None, None, "ctx", None))
    return jax.shard_map(
        on_device, mesh=mesh, in_specs=in_specs, out_specs=out_specs, check_vma=False
    )
```

profile of v0, /device:TPU:1, one launch (start us, length us, event | category | flops | bytes accessed | tf_op | source)
XLA Modules:
  0.0 256.8 jit_solution(8461394061242989045)
XLA Ops:
  7.2 0.0 all-gather.2.cloned.1.call-start
  7.2 0.7 all-gather.2.cloned.1.call-update
  7.9 0.8 reduce_window_sum.23
  8.7 0.7 bitcast_subtract_fusion
  9.4 0.8 select_reduce_fusion.1
  10.3 0.1 add_minimum_fusion
  10.3 0.1 min.22
  10.4 18.2 %gather_fusion = bf16[512,8192]{1,0:T(8,128)(2,1)} fusion(bf16[256,8192]{1,0:T(8,128)(2,1)} %bitcast.28, s32[1024]{0:T(1024)S(1)} %pad_clamp_fusion.1), kind=kCustom, calls=%fused_computation | custom fusion | bytes 16779264 | tf_op jit(solution)/shard_map/jit(_take)/gather | solution.py:44
  28.6 0.1 compare_and_fusion
  28.7 0.1 iota_compare_fusion.3
  28.8 7.6 %select_select_fusion = bf16[8,64,8192]{2,1,0:T(8,128)(2,1)} fusion(bf16[8,64,8192]{2,1,0:T(8,128)(2,1)} %bitcast.29, pred[8,64]{1,0:T(8,128)(4,1)S(1)} %compare_and_fusion, pred[8,64]{1,0:T(8,128)(4,1)S(1)} %iota_compare_fusion.3), kind=kLoop, calls=%fused_computation.7 | loop fusion | flops 8388608 | bytes 16778240 | tf_op jit(solution)/shard_map/jit(_where)/select_n | solution.py:45
  36.4 6.3 %all-to-all-start = ((bf16[8,64,8192]{2,1,0:T(8,128)(2,1)}), bf16[8,64,8192]{2,1,0:T(8,128)(2,1)}, u32[]{:S(2)}, u32[]{:S(2)}) async-start(bf16[8,64,8192]{2,1,0:T(8,128)(2,1)} %select_select_fusion), calls=%async_computation | async-start | bytes 16777216 | tf_op jit(solution)/shard_map/all_to_all | solution.py:68
  42.7 0.2 dynamic-slice_reduce_fusion
  42.9 0.1 convert_reduce_fusion
  43.0 0.1 select_reduce_fusion.2
  43.1 93.4 %all-to-all-done = bf16[8,64,8192]{2,1,0:T(8,128)(2,1)} async-done(((bf16[8,64,8192]{2,1,0:T(8,128)(2,1)}), bf16[8,64,8192]{2,1,0:T(8,128)(2,1)}, u32[]{:S(2)}, u32[]{:S(2)}) %all-to-all-start) | async-done | bytes 8388640 | tf_op jit(solution)/shard_map/all_to_all | solution.py:68
  136.5 13.6 %gather_fusion.1 = bf16[256,8192]{1,0:T(8,128)(2,1)} fusion(bf16[512,8192]{1,0:T(8,128)(2,1)} %bitcast.7, s32[1024]{0:T(1024)S(1)} %pad_clamp_fusion), kind=kCustom, calls=%fused_computation.1 | custom fusion | bytes 8389632 | tf_op jit(solution)/shard_map/jit(_take)/gather | solution.py:54
  150.1 0.0 copy-start
  150.1 0.0 copy-start.1
  150.1 3.4 %fusion = f32[256]{0:T(256)S(1)} fusion(bf16[256,8192]{1,0:T(8,128)(2,1)} %gather_fusion.1, pred[256]{0:T(512)(128)(4,1)S(1)} %compare_and_fusion.1), kind=kLoop, calls=%fused_computation.4 | loop fusion | flops 8388352 | bytes 4195584 | tf_op jit(solution)/shard_map/reduce_sum | solution.py:32
  153.6 57.0 %all-gather.2.cloned.1.call-done = bf16[8192,2048]{1,0:T(8,128)(2,1)} async-done(((bf16[512,2048]{1,0:T(8,128)(2,1)}), bf16[8192,2048]{1,0:T(8,128)(2,1)}) %all-gather.2.cloned.1.call-update) | async-done | bytes 33554448 | tf_op jit(solution)/shard_map/all_gather | solution.py:75
  210.6 0.0 copy-done
  210.6 0.0 copy-done.1
  210.6 16.3 %fusion.13 = bf16[32,8,16,128]{3,1,2,0:T(8,128)(2,1)S(1)} fusion(bf16[8192,2048]{1,0:T(8,128)(2,1)} %all-gather.2.cloned.1.call-done, f32[8192]{0:T(1024)S(1)} %copy-done, f32[256]{0:T(256)S(1)} %add_rsqrt_fusion, bf16[256,8192]{1,0:T(8,128)(2,1)} %gather_fusion.1, pred[256]{0:T(512)(128)(4,1)S(1)} %compare_and_fusion.1, f32[2048]{0:T(1024)S(1)} %copy-done.1), kind=kOutput, calls=%fused_computation.15 | convolution fusion | flops 8601468928 | bytes 38839552 | tf_op jit(solution)/shard_map/dot_general | solution.py:73
  226.9 0.2 copy.14
  227.2 1.8 copy.12
  228.9 4.9 %all-to-all-start.1 = ((bf16[1,256,2,8,128]{4,2,1,0,3:T(2,128)(2,1)}), bf16[1,256,2,8,128]{4,2,1,0,3:T(2,128)(2,1)S(1)}, u32[]{:S(2)}, u32[]{:S(2)}) async-start(bf16[1,256,2,8,128]{4,2,1,0,3:T(2,128)(2,1)} %copy.12), calls=%async_computation.1 | async-start | bytes 2097152 | tf_op jit(solution)/shard_map/all_to_all | solution.py:81
  233.9 4.7 %bitcast_select_fusion = bf16[1,256,8192]{2,1,0:T(8,128)(2,1)} fusion(bf16[256,8192]{1,0:T(8,128)(2,1)} %gather_fusion.1, pred[256]{0:T(512)(128)(4,1)S(1)} %compare_and_fusion.1), kind=kLoop, calls=%fused_computation.9 | loop fusion | flops 2097152 | bytes 8388864 | tf_op jit(solution)/shard_map/jit(_take)/select_n | solution.py:54
  238.5 10.4 %all-to-all-done.1 = bf16[1,256,2,8,128]{4,2,1,0,3:T(2,128)(2,1)S(1)} async-done(((bf16[1,256,2,8,128]{4,2,1,0,3:T(2,128)(2,1)}), bf16[1,256,2,8,128]{4,2,1,0,3:T(2,128)(2,1)S(1)}, u32[]{:S(2)}, u32[]{:S(2)}) %all-to-all-start.1) | async-done | bytes 1048608 | tf_op jit(solution)/shard_map/all_to_all | solution.py:81
  249.0 1.0 copy.16
  (10 shorter events, 0.1 us)
Async XLA Ops:
  7.2 203.4 %all-gather.2.cloned.1.call-start = ((), (), s32[]{:S(2)}) async-start(), calls=%async_computation.2 | async-start | bytes 35651584 | tf_op jit(solution)/shard_map/all_gather | solution.py:75
  36.4 100.2 %all-to-all-start = ((bf16[8,64,8192]{2,1,0:T(8,128)(2,1)}), bf16[8,64,8192]{2,1,0:T(8,128)(2,1)}, u32[]{:S(2)}, u32[]{:S(2)}) async-start(bf16[8,64,8192]{2,1,0:T(8,128)(2,1)} %select_select_fusion), calls=%async_computation | async-start | bytes 16777216 | tf_op jit(solution)/shard_map/all_to_all | solution.py:68
  150.1 60.5 %copy-start = (f32[8192]{0:T(1024)S(1)}, f32[8192]{0:T(1024)}, u32[]{:S(2)}) copy-start(f32[8192]{0:T(1024)} %param.9) | copy-start | bytes 98308
  150.1 60.5 %copy-start.1 = (f32[2048]{0:T(1024)S(1)}, f32[2048]{0:T(1024)}, u32[]{:S(2)}) copy-start(f32[2048]{0:T(1024)} %param.11) | copy-start | bytes 24580
  228.9 20.0 %all-to-all-start.1 = ((bf16[1,256,2,8,128]{4,2,1,0,3:T(2,128)(2,1)}), bf16[1,256,2,8,128]{4,2,1,0,3:T(2,128)(2,1)S(1)}, u32[]{:S(2)}, u32[]{:S(2)}) async-start(bf16[1,256,2,8,128]{4,2,1,0,3:T(2,128)(2,1)} %copy.12), calls=%async_computation.1 | async-start | bytes 2097152 | tf_op jit(solution)/shard_map/all_to_all | solution.py:81
Sparse Core Ops, SparseCore 0:
  10.1 200.4 all-gather.1
where the time goes:
time: 257 us
  waiting for transfers between devices  162 us (63%)
  local copies, waits for them, and re-layouts  35.1 us (14%)
  other arithmetic  18.5 us (7%)
  matrix products  16.3 us (6%)
  between operations  14.1 us (5%)
  starting transfers between devices  11.3 us (4%)
    all_to_all x1, waiting for transfers between devices, on_device(): lax.all_to_all(outgoing, 'ctx', split_axis=0, concat_axis=0, tiled=True)  93.4 us
    all_gather x1, waiting for transfers between devices, on_device(): lax.all_gather(kv_weight, 'dp', axis=0, tiled=True)  57 us
    gather x1, local copies, waits for them, and re-layouts, pack_document_runs(): jnp.take(rows, wanted.reshape(-1), axis=0).reshape(peer_count, capacity, -1)  18.2 us
    dot_general x1, matrix products, on_device(): jnp.dot(normed, lax.all_gather(kv_weight, 'dp', axis=0, tiled=True), pref...  16.3 us
    gather x1, local copies, waits for them, and re-layouts, unpack_runs(): return jnp.take(flat_rows, source * capacity + within, axis=0)  13.6 us
    all_to_all x1, waiting for transfers between devices, on_device(): lax.all_to_all(mapped_outputs, 'ctx', split_axis=3, concat_axis=1, tiled=...  10.4 us
    select_n x1, other arithmetic, pack_document_runs(): return jnp.where(is_live[:, :, None], picked, jnp.zeros_like(picked))  7.59 us
    all_to_all x1, starting transfers between devices, on_device(): lax.all_to_all(outgoing, 'ctx', split_axis=0, concat_axis=0, tiled=True)  6.29 us
  transfers between devices with their start and end apart: 3, of which 3 were waited for; matrix products, arithmetic and copies ran while one was open for 20% of the time, Pallas kernels for 0%

commit v1 on v0

--- a/solution.py
+++ b/solution.py
@@ -72,7 +72,9 @@
     normed = rms_normed(moved_rows, norm_gain)
     summed_squares = jnp.dot(
         normed,
-        lax.all_gather(kv_weight, "dp", axis=0, tiled=True),
+        jnp.concatenate(
+            lax.all_to_all(jnp.stack([kv_weight] * lax.axis_size("dp")), "dp", 0, 0), axis=0
+        ),
         preferred_element_type=jnp.float32,
     )
     mapped_outputs = (

time: 257 us -> 811 us (3.16)
  waiting for transfers between devices: 162 us -> 611 us
  blocking collectives: 0 us -> 102 us
  between operations: 14.1 us -> 0.71 us
  local copies, waits for them, and re-layouts: 35.1 us -> 45.9 us
    all_to_all x1, waiting for transfers between devices: 93.4 us -> 600 us  [on_device(): lax.all_to_all(jnp.stack([kv_weight] * lax.axis_size('dp')), 'dp', 0, 0)]
    all_to_all x0 -> x1, blocking collectives: none -> 102 us  [on_device(): lax.all_to_all(outgoing, 'ctx', split_axis=0, concat_axis=0, tiled=True)]
    all_gather x1 -> x0, waiting for transfers between devices: 57 us -> none  [on_device(): lax.all_gather(kv_weight, 'dp', axis=0, tiled=True)]
    another operation x0 -> x1, local copies, waits for them, and re-layouts: none -> 10.9 us  [on_device(): jnp.stack([kv_weight] * lax.axis_size('dp'))]
  transfers between devices with their start and end apart: 3 -> 2, of which waited for: 3 -> 2; matrix products, arithmetic and copies ran while one was open for 20% -> 3% of each run, Pallas kernels for 0% -> 0%
where the time goes in v1:
time: 811 us; the launch traced here: 808 us
  waiting for transfers between devices  611 us (75%)
  blocking collectives  102 us (13%)
  local copies, waits for them, and re-layouts  45.9 us (6%)
  other arithmetic  18.5 us (2%)
  matrix products  16.3 us (2%)
  starting transfers between devices  14 us (2%)
    all_to_all x1, waiting for transfers between devices, on_device(): lax.all_to_all(jnp.stack([kv_weight] * lax.axis_size('dp')), 'dp', 0, 0)  600 us
    all_to_all x1, blocking collectives, on_device(): lax.all_to_all(outgoing, 'ctx', split_axis=0, concat_axis=0, tiled=True)  102 us
    gather x1, local copies, waits for them, and re-layouts, pack_document_runs(): jnp.take(rows, wanted.reshape(-1), axis=0).reshape(peer_count, capacity, -1)  18.2 us
    dot_general x1, matrix products, on_device(): jnp.dot(normed, jnp.concatenate(lax.all_to_all(jnp.stack([kv_weight] * la...  16.3 us
  transfers between devices with their start and end apart: 2, of which 2 were waited for; matrix products, arithmetic and copies ran while one was open for 3% of the time, Pallas kernels for 0%

profile of v1, /device:TPU:1, one launch (start us, length us, event | category | flops | bytes accessed | tf_op | source)
XLA Modules:
  0.0 808.2 jit_solution(120070301312632093)
XLA Ops:
  0.6 0.8 reduce_window_sum.23
  1.5 0.7 bitcast_subtract_fusion
  2.2 0.8 select_reduce_fusion.1
  3.0 0.1 add_minimum_fusion
  3.1 0.1 compare_and_fusion
  3.1 0.1 min.22
  3.2 0.1 iota_compare_fusion.3
  3.3 18.2 %gather_fusion = bf16[512,8192]{1,0:T(8,128)(2,1)} fusion(bf16[256,8192]{1,0:T(8,128)(2,1)} %bitcast.29, s32[1024]{0:T(1024)S(1)} %pad_clamp_fusion.1), kind=kCustom, calls=%fused_computation | custom fusion | bytes 16779264 | tf_op jit(solution)/shard_map/jit(_take)/gather | solution.py:44
  21.5 7.6 select_select_fusion
  29.1 0.0 copy-start
  29.1 102.2 %all_to_all.28 = bf16[8,64,8192]{2,1,0:T(8,128)(2,1)} all-to-all(bf16[8,64,8192]{2,1,0:T(8,128)(2,1)} %select_select_fusion), channel_id=1, replica_groups=mesh['dp'=16,'ctx'=8] {'ctx'}, dimensions={0} | all-to-all | bytes 16777216 | tf_op jit(solution)/shard_map/all_to_all | solution.py:68
  131.3 0.0 copy-done
  131.3 10.9 %stack.2 = bf16[16,512,2048]{2,1,0:T(8,128)(2,1)} broadcast(bf16[512,2048]{1,0:T(8,128)(2,1)S(1)} %copy-done), dimensions={1,2} | broadcast | bytes 35651584 | tf_op jit(solution)/shard_map/stack | solution.py:76
  142.2 7.9 all-to-all-start.1
  150.2 0.2 dynamic-slice_reduce_fusion
  150.4 0.1 convert_reduce_fusion
  150.5 0.1 select_reduce_fusion.2
  150.6 13.5 %gather_fusion.1 = bf16[256,8192]{1,0:T(8,128)(2,1)} fusion(bf16[512,8192]{1,0:T(8,128)(2,1)} %bitcast.30, s32[1024]{0:T(1024)S(1)} %pad_clamp_fusion), kind=kCustom, calls=%fused_computation.1 | custom fusion | bytes 8389632 | tf_op jit(solution)/shard_map/jit(_take)/gather | solution.py:54
  164.1 0.0 copy-start.1
  164.1 0.0 copy-start.2
  164.1 3.4 fusion
  167.5 600.2 %all-to-all-done.1 = bf16[16,512,2048]{2,1,0:T(8,128)(2,1)} async-done(((bf16[16,512,2048]{2,1,0:T(8,128)(2,1)}), bf16[16,512,2048]{2,1,0:T(8,128)(2,1)}, u32[]{:S(2)}, u32[]{:S(2)}) %all-to-all-start.1) | async-done | bytes 33554464 | tf_op jit(solution)/shard_map/all_to_all | solution.py:76
  767.7 0.0 copy-done.1
  767.7 0.0 copy-done.2
  767.7 16.3 %fusion.13 = bf16[32,8,16,128]{3,1,2,0:T(8,128)(2,1)S(1)} fusion(bf16[8192,2048]{1,0:T(8,128)(2,1)} %bitcast.12, f32[8192]{0:T(1024)S(1)} %copy-done.1, f32[256]{0:T(256)S(1)} %add_rsqrt_fusion, bf16[256,8192]{1,0:T(8,128)(2,1)} %gather_fusion.1, pred[256]{0:T(512)(128)(4,1)S(1)} %compare_and_fusion.1, f32[2048]{0:T(1024)S(1)} %copy-done.2), kind=kOutput, calls=%fused_computation.15 | convolution fusion | flops 8601468928 | bytes 38839552 | tf_op jit(solution)/shard_map/dot_general | solution.py:73
  784.1 0.2 copy.14
  784.3 1.8 copy.12
  786.1 6.1 all-to-all-start.2
  792.1 4.7 bitcast_select_fusion
  796.8 10.4 %all-to-all-done.2 = bf16[1,256,2,8,128]{4,2,1,0,3:T(2,128)(2,1)S(1)} async-done(((bf16[1,256,2,8,128]{4,2,1,0,3:T(2,128)(2,1)}), bf16[1,256,2,8,128]{4,2,1,0,3:T(2,128)(2,1)S(1)}, u32[]{:S(2)}, u32[]{:S(2)}) %all-to-all-start.2) | async-done | bytes 1048608 | tf_op jit(solution)/shard_map/all_to_all | solution.py:83
  807.2 1.0 copy.16
  (10 shorter events, 0.1 us)
Async XLA Ops:
  29.1 102.2 %copy-start = (bf16[512,2048]{1,0:T(8,128)(2,1)S(1)}, bf16[512,2048]{1,0:T(8,128)(2,1)}, u32[]{:S(2)}) copy-start(bf16[512,2048]{1,0:T(8,128)(2,1)} %param.10) | copy-start | bytes 6291460
  142.2 625.5 %all-to-all-start.1 = ((bf16[16,512,2048]{2,1,0:T(8,128)(2,1)}), bf16[16,512,2048]{2,1,0:T(8,128)(2,1)}, u32[]{:S(2)}, u32[]{:S(2)}) async-start(bf16[16,512,2048]{2,1,0:T(8,128)(2,1)} %stack.2), calls=%async_computation.1 | async-start | bytes 67108864 | tf_op jit(solution)/shard_map/all_to_all | solution.py:76
  164.1 603.6 %copy-start.1 = (f32[8192]{0:T(1024)S(1)}, f32[8192]{0:T(1024)}, u32[]{:S(2)}) copy-start(f32[8192]{0:T(1024)} %param.9) | copy-start | bytes 98308
  164.1 603.6 %copy-start.2 = (f32[2048]{0:T(1024)S(1)}, f32[2048]{0:T(1024)}, u32[]{:S(2)}) copy-start(f32[2048]{0:T(1024)} %param.11) | copy-start | bytes 24580
  786.1 21.2 %all-to-all-start.2 = ((bf16[1,256,2,8,128]{4,2,1,0,3:T(2,128)(2,1)}), bf16[1,256,2,8,128]{4,2,1,0,3:T(2,128)(2,1)S(1)}, u32[]{:S(2)}, u32[]{:S(2)}) async-start(bf16[1,256,2,8,128]{4,2,1,0,3:T(2,128)(2,1)} %copy.12), calls=%async_computation.2 | async-start | bytes 2097152 | tf_op jit(solution)/shard_map/all_to_all | solution.py:83
